TPU v7x, 32 devices: a whole 2x2x4 slice. The times are simulated.
32 devices in a mesh: grp: 4 (over y, x), node: 8 (over z, core).
Axes of the slice: x: 2, y: 2, z: 4, core: 2. Of those that a mesh axis runs over, the one named last changes fastest.
Arguments:
- coefficients: float32 [8192, 1024], P(('grp', 'node')), may hold values from -6 to 6
- transfer: float32 [5, 8192, 512], P(None, ('grp', 'node')), may hold values from -0.3125 to 0.3125
- ranks: int32 [5, 32], P(None, ('grp', 'node')), may hold values from 128 to 256, as said below
Outputs:
- applied: float32 [8192, 1024], P(('grp', 'node'))
Inputs may be any that keep to these rules, and one draw needn't show every extreme that they name: `ranks`: in each level some block has rank exactly 256 and some block rank 256 // 2.
All inputs are finite; a program needn't handle non-finite values.
Results may differ from a plain program's by a relative error of at most 0.00011.
Values sent between devices are 32-bit elements; how exact they have to be, the bound alone decides.
A program may use at most 128 MiB of HBM per device.

v0:
```python
import functools

import jax
import jax.numpy as jnp
from jax import lax
from jax.experimental import pallas as pl
from jax.experimental.pallas import tpu as pltpu
from jax.sharding import PartitionSpec as P

LANES = 128


def split_cols(x):
    high = x.astype(jnp.bfloat16)
    low = (x - high.astype(jnp.float32)).astype(jnp.bfloat16)
    return high, low


def plan(node_bits, group_bits):
    levels, due = [], 0
    for bit in range(node_bits):
        due += 3 if bit else 0
        levels.append(("node", bit, due))
    for bit in range(group_bits):
        due += 2
        levels.append(("grp", bit, due))
    return levels


def kernel(
    levels, ranks_ref, coef_ref, transfer_ref, out_ref,
    raw, mats, own_wide, own, first, landed, mixed, stage,
    raw_sem, stage_sem, first_send, first_recv, send_sem, recv_sem,
):
    depth = coef_ref.shape[0]
    chunks, _, width = first.shape
    pieces, short, _ = landed.shape[1:]
    half = width // 2
    count = len(levels)

    places, partners = [], []
    for axis, bit, _ in levels:
        place = lax.axis_index(axis)
        upper = (place // 2**bit) % 2
        places.append(upper)
        partners.append({axis: place + (1 - 2 * upper) * 2**bit})

    def cols(chunk):
        return pl.ds(pl.multiple_of(chunk * width, width), width)

    def load_chunk(chunk):
        return pltpu.make_async_copy(
            coef_ref.at[:, cols(chunk)], stage.at[chunk], stage_sem.at[chunk]
        )

    def load_matrix(level):
        return pltpu.make_async_copy(transfer_ref.at[level], raw.at[level], raw_sem.at[level])

    def send_first(chunk):
        return pltpu.make_async_remote_copy(
            src_ref=coef_ref.at[:, cols(chunk)],
            dst_ref=first.at[chunk],
            send_sem=first_send.at[chunk],
            recv_sem=first_recv.at[chunk],
            device_id=partners[0],
            device_id_type=pl.DeviceIdType.MESH,
        )

    def send(level, piece):
        return pltpu.make_async_remote_copy(
            src_ref=mixed.at[level - 1, piece],
            dst_ref=landed.at[level - 1, piece],
            send_sem=send_sem.at[level - 1, piece],
            recv_sem=recv_sem.at[level - 1, piece],
            device_id=partners[level],
            device_id_type=pl.DeviceIdType.MESH,
        )

    barrier = pltpu.get_barrier_semaphore()
    for level in range(count):
        pl.semaphore_signal(
            barrier, inc=1, device_id=partners[level], device_id_type=pl.DeviceIdType.MESH
        )
    load_matrix(0).start()
    for chunk in range(chunks):
        load_chunk(chunk).start()
    for level in range(1, count):
        load_matrix(level).start()
    pl.semaphore_wait(barrier, count)
    for chunk in range(chunks):
        send_first(chunk).start()

    left_lanes = lax.broadcasted_iota(jnp.int32, (short, width), 1) < half

    def turn(x):
        return pltpu.roll(x, half, 1)

    def prepare(level):
        load_matrix(level).wait()
        keep = lax.broadcasted_iota(jnp.int32, (depth, depth), 0) < ranks_ref[0, level]
        for side, place in enumerate((places[level], 1 - places[level])):
            block = raw[level, :, pl.ds(pl.multiple_of(place * depth, depth), depth)]
            high, low = split_cols(jnp.where(keep, block, jnp.zeros_like(block)))
            mats[level, :depth, side * depth:(side + 1) * depth] = high
            mats[level, depth:, side * depth:(side + 1) * depth] = low

    def mix(level, mine, other):
        total = jnp.dot(
            mats[level, :, :depth], mine, preferred_element_type=jnp.float32
        ) + jnp.dot(mats[level, :, depth:], other, preferred_element_type=jnp.float32)
        return total[:depth] + total[depth:]

    def spread(top, bottom):
        both = []
        for x in (top, bottom):
            high = x.astype(jnp.bfloat16).astype(jnp.float32)
            both.append(jnp.where(left_lanes, high, x - high).astype(jnp.bfloat16))
        return jnp.concatenate(both, axis=0)

    def spread_packed(packed):
        turned = turn(packed)
        top = jnp.where(left_lanes, packed, turned)
        bottom = jnp.where(left_lanes, turned, packed)
        return spread(top, bottom)

    def task_first(chunk):
        load_chunk(chunk).wait()
        own_wide[...] = jnp.concatenate(split_cols(stage[chunk]), axis=1)
        send_first(chunk).wait_recv()
        total = mix(0, own_wide[...], jnp.concatenate(split_cols(first[chunk]), axis=1))
        result = total[:, :width] + total[:, width:]
        top, bottom = result[:short], result[short:]
        packs = (
            jnp.where(left_lanes, top, turn(bottom)),
            jnp.where(left_lanes, turn(top), bottom),
        )
        for side, packed in enumerate(packs):
            piece = 2 * chunk + side
            mixed[0, piece] = packed
            own[piece] = spread_packed(packed)
            send(1, piece).start()

    def task(level, piece):
        send(level, piece).wait_recv()
        total = mix(level, own[piece], spread_packed(landed[level - 1, piece]))
        result = total + turn(total)
        if level + 1 < count:
            top, bottom = result[:short], result[short:]
            mixed[level, piece] = jnp.where(left_lanes, top, bottom)
            own[piece] = spread(top, bottom)
            send(level + 1, piece).start()
        else:
            here = cols(piece // 2)
            lanes = lax.broadcasted_iota(jnp.int32, (depth, width), 1)
            out_ref[:, here] = jnp.where(lanes < half * (piece % 2), out_ref[:, here], result)

    prepare(0)

    def step(s, carry):
        @pl.when((s % 2 == 0) & (s < pieces))
        def _():
            task_first(s // 2)

        for level, (_, _, due) in enumerate(levels):
            if level:
                @pl.when((s >= due) & (s < due + pieces))
                def _():
                    task(level, s - due)

            if level + 1 < count:
                @pl.when(s == due)
                def _():
                    prepare(level + 1)
        return carry

    lax.fori_loop(0, levels[-1][2] + pieces, step, 0)

    def finish(piece, carry):
        for level in range(1, count):
            send(level, piece).wait_send()
        return carry

    lax.fori_loop(0, pieces, finish, 0)

    def finish_first(chunk, carry):
        send_first(chunk).wait_send()
        return carry

    lax.fori_loop(0, chunks, finish_first, 0)


def per_device(coefficients, transfer, ranks):
    levels = plan(
        lax.axis_size("node").bit_length() - 1, lax.axis_size("grp").bit_length() - 1
    )
    count = len(levels)
    depth, width = coefficients.shape
    chunks = width // LANES
    pieces = 2 * chunks
    short = depth // 2
    call = pl.pallas_call(
        functools.partial(kernel, levels),
        out_shape=jax.ShapeDtypeStruct(coefficients.shape, jnp.float32),
        in_specs=[
            pl.BlockSpec(memory_space=pltpu.SMEM),
            pl.BlockSpec(memory_space=pltpu.HBM),
            pl.BlockSpec(memory_space=pltpu.HBM),
        ],
        out_specs=pl.BlockSpec(memory_space=pltpu.VMEM),
        scratch_shapes=[
            pltpu.VMEM((count, depth, 2 * depth), jnp.float32),
            pltpu.VMEM((count, 2 * depth, 2 * depth), jnp.bfloat16),
            pltpu.VMEM((depth, 2 * LANES), jnp.bfloat16),
            pltpu.VMEM((pieces, depth, LANES), jnp.bfloat16),
            pltpu.VMEM((chunks, depth, LANES), jnp.float32),
            pltpu.VMEM((count - 1, pieces, short, LANES), jnp.float32),
            pltpu.VMEM((count - 1, pieces, short, LANES), jnp.float32),
            pltpu.VMEM((chunks, depth, LANES), jnp.float32),
            pltpu.SemaphoreType.DMA((count,)),
            pltpu.SemaphoreType.DMA((chunks,)),
            pltpu.SemaphoreType.DMA((chunks,)),
            pltpu.SemaphoreType.DMA((chunks,)),
            pltpu.SemaphoreType.DMA((count - 1, pieces)),
            pltpu.SemaphoreType.DMA((count - 1, pieces)),
        ],
        compiler_params=pltpu.CompilerParams(
            collective_id=0, has_side_effects=True, vmem_limit_bytes=55_000_000
        ),
        name="butterfly",
    )
    return call(ranks.T, coefficients, transfer)


def solution(mesh):
    return jax.shard_map(
        per_device,
        mesh=mesh,
        in_specs=(
            P(("grp", "node"), None),
            P(None, ("grp", "node"), None),
            P(None, ("grp", "node")),
        ),
        out_specs=P(("grp", "node"), None),
        check_vma=False,
    )
```

profile of v0, /device:TPU:0, one launch (start us, length us, event | category | flops | bytes accessed | tf_op | source)
XLA Modules:
  0.0 70.6 jit_solution(2417196065949195804)
XLA Ops:
  0.0 0.0 copy-start
  0.0 0.7 copy-done
  0.7 69.0 %butterfly.1 = f32[256,1024]{1,0:T(8,128)S(1)} custom-call(s32[1,5]{1,0:T(1,128)S(1)} %bitcast.1, f32[256,1024]{1,0:T(8,128)} %coef_ref.1, f32[5,256,512]{2,1,0:T(8,128)} %transfer_ref.1), custom_call_target="tpu_custom_call" | custom-call | tf_op jit(solution)/shard_map/butterfly/pallas_call | solution.py:231
  69.7 1.0 %copy.5 = f32[256,1024]{1,0:T(8,128)} copy(f32[256,1024]{1,0:T(8,128)S(1)} %butterfly.1) | data formatting | bytes 2097152
Async XLA Ops:
  0.0 0.7 copy-start
where the time goes:
time: 70.8 us; the launch traced here: 70.6 us
  Pallas kernels  69 us (97%)
  local copies, waits for them, and re-layouts  1.63 us (2%)
    pallas_call x1, Pallas kernels, per_device(): return call(ranks.T, coefficients, transfer)  69 us
    unnamed x3, local copies, waits for them, and re-layouts  1.63 us

commit v1 on v0

v1 whole, which is shorter than its diff:
```python
import functools

import jax
import jax.numpy as jnp
from jax import lax
from jax.experimental import pallas as pl
from jax.experimental.pallas import tpu as pltpu
from jax.sharding import PartitionSpec as P

LANES = 128
UNIT = 32
EDGE = LANES // UNIT
LAGS = ((6, 6, 4), (6, 4, 4))


def split_rows(x):
    high = x.astype(jnp.bfloat16)
    low = (x - high.astype(jnp.float32)).astype(jnp.bfloat16)
    return jnp.concatenate([high, low], axis=0)


def plan(node_bits, group_bits):
    levels, due = [], (0, 0)
    for bit in range(node_bits):
        if bit:
            due = tuple(d + lag[min(bit, 2) - 1] for d, lag in zip(due, LAGS))
        levels.append(("node", bit, due))
    for bit in range(group_bits):
        due = tuple(d + lag[2] for d, lag in zip(due, LAGS))
        levels.append(("grp", bit, due))
    return levels


def kernel(
    levels, ranks_ref, coef_ref, transfer_ref, out_ref,
    raw, mats, stage, first, own, given, landed, mixed, done,
    raw_sem, stage_sem, first_send, first_recv, send_sem, recv_sem,
):
    depth, columns = coef_ref.shape
    chunks = columns // LANES
    units = columns // UNIT
    count = len(levels)

    places, partners = [], []
    for axis, bit, _ in levels:
        place = lax.axis_index(axis)
        upper = (place // 2**bit) % 2
        places.append(upper)
        partners.append({axis: place + (1 - 2 * upper) * 2**bit})
    outer = (places[1] + places[2] + 1) % 2
    dues = [inner + outer * (outside - inner) for _, _, (inner, outside) in levels]

    def cols(chunk):
        return pl.ds(pl.multiple_of(chunk * LANES, LANES), LANES)

    def load_chunk(chunk):
        return pltpu.make_async_copy(
            coef_ref.at[:, cols(chunk)], stage.at[chunk], stage_sem.at[chunk]
        )

    def load_matrix(level):
        return pltpu.make_async_copy(transfer_ref.at[level], raw.at[level], raw_sem.at[level])

    def send_first(chunk):
        return pltpu.make_async_remote_copy(
            src_ref=coef_ref.at[:, cols(chunk)],
            dst_ref=first.at[chunk],
            send_sem=first_send,
            recv_sem=first_recv.at[chunk],
            device_id=partners[0],
            device_id_type=pl.DeviceIdType.MESH,
        )

    def send(level, unit, rows):
        return pltpu.make_async_remote_copy(
            src_ref=mixed.at[level - 1, rows],
            dst_ref=landed.at[level - 1, rows],
            send_sem=send_sem.at[level - 1],
            recv_sem=recv_sem.at[level - 1, unit],
            device_id=partners[level],
            device_id_type=pl.DeviceIdType.MESH,
        )

    load_matrix(0).start()
    load_chunk(0).start()
    barrier = pltpu.get_barrier_semaphore()
    for level in range(count):
        pl.semaphore_signal(
            barrier, inc=1, device_id=partners[level], device_id_type=pl.DeviceIdType.MESH
        )
    load_chunk(1).start()
    load_matrix(1).start()
    pl.semaphore_wait(barrier, count)
    send_first(0).start()
    send_first(1).start()

    def prepare(level):
        load_matrix(level).wait()
        keep = lax.broadcasted_iota(jnp.int32, (depth, depth), 0) < ranks_ref[0, level]
        for side, place in enumerate((places[level], 1 - places[level])):
            block = raw[level, :, pl.ds(pl.multiple_of(place * depth, depth), depth)]
            both = split_rows(jnp.where(keep, block, jnp.zeros_like(block)).T)
            mats[level, 0, side * depth:(side + 1) * depth] = both[:depth]
            mats[level, 1, side * depth:(side + 1) * depth] = both[depth:]

    def mix(level, mine, other):
        total = None
        for part in range(2):
            for side, x in enumerate((mine, other)):
                term = jnp.dot(
                    x, mats[level, part, side * depth:(side + 1) * depth],
                    preferred_element_type=jnp.float32,
                )
                total = term if total is None else total + term
        half = total.shape[0] // 2
        return total[:half] + total[half:]

    def by_width(unit, body):
        inner = (unit >= EDGE) & (unit < units - EDGE)

        def run(start, width):
            start = pl.multiple_of(start, width)
            body(pl.ds(start, width), pl.ds(pl.multiple_of(2 * start, 2 * width), 2 * width))

        @pl.when(inner & (unit % 2 == 1))
        def _():
            run((unit - 1) * UNIT, 2 * UNIT)

        @pl.when(jnp.logical_not(inner))
        def _():
            run(unit * UNIT, UNIT)

    def spread(chunk, width):
        for source, target in ((stage, own), (first, given)):
            turned = source[chunk].T
            for start in range(0, LANES, width):
                where = pl.multiple_of(2 * (chunk * LANES + start), 2 * width)
                target[pl.ds(where, 2 * width)] = split_rows(turned[start:start + width])

    def open_chunk(chunk, width):
        @pl.when(chunk + 2 < chunks)
        def _():
            load_chunk(chunk + 2).start()
            send_first(chunk + 2).start()

        load_chunk(chunk).wait()
        send_first(chunk).wait_recv()
        spread(chunk, width)

    def task_first(unit):
        inner = (unit >= EDGE) & (unit < units - EDGE)

        @pl.when(inner & (unit % EDGE == 1))
        def _():
            open_chunk(unit // EDGE, 2 * UNIT)

        @pl.when(jnp.logical_not(inner) & (unit % EDGE == 0))
        def _():
            open_chunk(unit // EDGE, UNIT)

        def body(rows, twice):
            result = mix(0, own[twice], given[twice])
            mixed[0, rows] = result
            own[twice] = split_rows(result)
            send(1, unit, rows).start()

        by_width(unit, body)

    def task(level, unit):
        def body(rows, twice):
            send(level, unit, rows).wait_recv()
            result = mix(level, own[twice], split_rows(landed[level - 1, rows]))
            if level + 1 < count:
                mixed[level, rows] = result
                own[twice] = split_rows(result)
                send(level + 1, unit, rows).start()
            else:
                done[rows] = result

        by_width(unit, body)
        if level + 1 == count:
            @pl.when(unit % EDGE == EDGE - 1)
            def _():
                chunk = unit // EDGE
                out_ref[:, cols(chunk)] = done[cols(chunk)].T

    prepare(0)

    def step(s, carry):
        @pl.when(s < units)
        def _():
            task_first(s)

        @pl.when(s == 0)
        def _():
            for level in range(2, count):
                load_matrix(level).start()

        for level, due in enumerate(dues):
            if level:
                @pl.when((s >= due) & (s < due + units))
                def _():
                    task(level, s - due)

            if level + 1 < count:
                @pl.when(s == due + 1)
                def _():
                    prepare(level + 1)
        return carry

    lax.fori_loop(0, dues[-1] + units, step, 0)

    for level in range(1, count):
        pltpu.make_async_copy(
            mixed.at[level - 1], mixed.at[level - 1], send_sem.at[level - 1]
        ).wait()
    pltpu.make_async_copy(coef_ref, coef_ref, first_send).wait()


def per_device(coefficients, transfer, ranks):
    levels = plan(
        lax.axis_size("node").bit_length() - 1, lax.axis_size("grp").bit_length() - 1
    )
    count = len(levels)
    depth, columns = coefficients.shape
    chunks = columns // LANES
    units = columns // UNIT
    call = pl.pallas_call(
        functools.partial(kernel, levels),
        out_shape=jax.ShapeDtypeStruct(coefficients.shape, jnp.float32),
        in_specs=[
            pl.BlockSpec(memory_space=pltpu.SMEM),
            pl.BlockSpec(memory_space=pltpu.HBM),
            pl.BlockSpec(memory_space=pltpu.HBM),
        ],
        out_specs=pl.BlockSpec(memory_space=pltpu.VMEM),
        scratch_shapes=[
            pltpu.VMEM((count, depth, 2 * depth), jnp.float32),
            pltpu.VMEM((count, 2, 2 * depth, depth), jnp.bfloat16),
            pltpu.VMEM((chunks, depth, LANES), jnp.float32),
            pltpu.VMEM((chunks, depth, LANES), jnp.float32),
            pltpu.VMEM((2 * columns, depth), jnp.bfloat16),
            pltpu.VMEM((2 * columns, depth), jnp.bfloat16),
            pltpu.VMEM((count - 1, columns, depth), jnp.float32),
            pltpu.VMEM((count - 1, columns, depth), jnp.float32),
            pltpu.VMEM((columns, depth), jnp.float32),
            pltpu.SemaphoreType.DMA((count,)),
            pltpu.SemaphoreType.DMA((chunks,)),
            pltpu.SemaphoreType.DMA,
            pltpu.SemaphoreType.DMA((chunks,)),
            pltpu.SemaphoreType.DMA((count - 1,)),
            pltpu.SemaphoreType.DMA((count - 1, units)),
        ],
        compiler_params=pltpu.CompilerParams(
            collective_id=0, has_side_effects=True, vmem_limit_bytes=55_000_000
        ),
        name="butterfly",
    )
    return call(ranks.T, coefficients, transfer)


def solution(mesh):
    return jax.shard_map(
        per_device,
        mesh=mesh,
        in_specs=(
            P(("grp", "node"), None),
            P(None, ("grp", "node"), None),
            P(None, ("grp", "node")),
        ),
        out_specs=P(("grp", "node"), None),
        check_vma=False,
    )
```

time: 70.8 us -> 68 us (0.960)
  Pallas kernels: 69 us -> 66.2 us
    pallas_call x1, Pallas kernels: 69 us -> 66.2 us  [per_device(): return call(ranks.T, coefficients, transfer)]
where the time goes in v1:
time: 68 us; the launch traced here: 67.8 us
  Pallas kernels  66.2 us (97%)
  local copies, waits for them, and re-layouts  1.63 us (2%)
    pallas_call x1, Pallas kernels, per_device(): return call(ranks.T, coefficients, transfer)  66.2 us
    unnamed x3, local copies, waits for them, and re-layouts  1.63 us

profile of v1, /device:TPU:0, one launch (start us, length us, event | category | flops | bytes accessed | tf_op | source)
XLA Modules:
  0.0 67.8 jit_solution(13285930546995462992)
XLA Ops:
  0.0 0.0 copy-start
  0.0 0.7 copy-done
  0.7 66.2 %butterfly.1 = f32[256,1024]{1,0:T(8,128)S(1)} custom-call(s32[1,5]{1,0:T(1,128)S(1)} %bitcast.1, f32[256,1024]{1,0:T(8,128)} %coef_ref.1, f32[5,256,512]{2,1,0:T(8,128)} %transfer_ref.1), custom_call_target="tpu_custom_call" | custom-call | tf_op jit(solution)/shard_map/butterfly/pallas_call | solution.py:259
  66.8 1.0 %copy.5 = f32[256,1024]{1,0:T(8,128)} copy(f32[256,1024]{1,0:T(8,128)S(1)} %butterfly.1) | data formatting | bytes 2097152
Async XLA Ops:
  0.0 0.7 copy-start

commit v2 on v1

--- a/solution.py
+++ b/solution.py
@@ -33,11 +33,10 @@
 
 def kernel(
     levels, ranks_ref, coef_ref, transfer_ref, out_ref,
-    raw, mats, stage, first, own, given, landed, mixed, done,
-    raw_sem, stage_sem, first_send, first_recv, send_sem, recv_sem,
+    limits, raw, mats, stage, first, own, given, landed, mixed, done,
+    limits_sem, raw_sem, stage_sem, first_send, first_recv, send_sem, recv_sem,
 ):
     depth, columns = coef_ref.shape
-    chunks = columns // LANES
     units = columns // UNIT
     count = len(levels)
 
@@ -53,50 +52,61 @@
     def cols(chunk):
         return pl.ds(pl.multiple_of(chunk * LANES, LANES), LANES)
 
-    def load_chunk(chunk):
+    parts = [pl.ds(0, LANES), pl.ds(LANES, LANES), pl.ds(2 * LANES, columns - 2 * LANES)]
+
+    def load_part(part):
         return pltpu.make_async_copy(
-            coef_ref.at[:, cols(chunk)], stage.at[chunk], stage_sem.at[chunk]
+            coef_ref.at[:, parts[part]], stage.at[:, parts[part]], stage_sem.at[part]
         )
 
     def load_matrix(level):
         return pltpu.make_async_copy(transfer_ref.at[level], raw.at[level], raw_sem.at[level])
 
-    def send_first(chunk):
+    def send_first(part):
         return pltpu.make_async_remote_copy(
-            src_ref=coef_ref.at[:, cols(chunk)],
-            dst_ref=first.at[chunk],
+            src_ref=coef_ref.at[:, parts[part]],
+            dst_ref=first.at[:, parts[part]],
             send_sem=first_send,
-            recv_sem=first_recv.at[chunk],
+            recv_sem=first_recv.at[part],
             device_id=partners[0],
             device_id_type=pl.DeviceIdType.MESH,
         )
+
+    def slot(unit):
+        late = unit // (units - EDGE)
+        early = 1 - (unit + units - EDGE) // units
+        narrow = early + late
+        return narrow * (unit - late * (units // 2 - EDGE)) + (1 - narrow) * (EDGE // 2 + unit // 2)
 
     def send(level, unit, rows):
         return pltpu.make_async_remote_copy(
             src_ref=mixed.at[level - 1, rows],
             dst_ref=landed.at[level - 1, rows],
-            send_sem=send_sem.at[level - 1],
-            recv_sem=recv_sem.at[level - 1, unit],
+            send_sem=send_sem,
+            recv_sem=recv_sem.at[level - 1, slot(unit)],
             device_id=partners[level],
             device_id_type=pl.DeviceIdType.MESH,
         )
 
+    load_limits = pltpu.make_async_copy(ranks_ref, limits, limits_sem)
+    load_limits.start()
     load_matrix(0).start()
-    load_chunk(0).start()
+    load_part(0).start()
     barrier = pltpu.get_barrier_semaphore()
     for level in range(count):
         pl.semaphore_signal(
             barrier, inc=1, device_id=partners[level], device_id_type=pl.DeviceIdType.MESH
         )
-    load_chunk(1).start()
+    load_part(1).start()
+    pl.semaphore_wait(barrier, count)
+    for part in range(len(parts)):
+        send_first(part).start()
     load_matrix(1).start()
-    pl.semaphore_wait(barrier, count)
-    send_first(0).start()
-    send_first(1).start()
+    load_part(2).start()
 
     def prepare(level):
         load_matrix(level).wait()
-        keep = lax.broadcasted_iota(jnp.int32, (depth, depth), 0) < ranks_ref[0, level]
+        keep = lax.broadcasted_iota(jnp.int32, (depth, depth), 0) < limits[0, level]
         for side, place in enumerate((places[level], 1 - places[level])):
             block = raw[level, :, pl.ds(pl.multiple_of(place * depth, depth), depth)]
             both = split_rows(jnp.where(keep, block, jnp.zeros_like(block)).T)
@@ -132,19 +142,18 @@
 
     def spread(chunk, width):
         for source, target in ((stage, own), (first, given)):
-            turned = source[chunk].T
+            turned = source[:, cols(chunk)].T
             for start in range(0, LANES, width):
                 where = pl.multiple_of(2 * (chunk * LANES + start), 2 * width)
                 target[pl.ds(where, 2 * width)] = split_rows(turned[start:start + width])
 
     def open_chunk(chunk, width):
-        @pl.when(chunk + 2 < chunks)
-        def _():
-            load_chunk(chunk + 2).start()
-            send_first(chunk + 2).start()
-
-        load_chunk(chunk).wait()
-        send_first(chunk).wait_recv()
+        for part in range(len(parts)):
+            @pl.when(chunk == part)
+            def _():
+                load_part(part).wait()
+                send_first(part).wait_recv()
+
         spread(chunk, width)
 
     def task_first(unit):
@@ -184,6 +193,7 @@
                 chunk = unit // EDGE
                 out_ref[:, cols(chunk)] = done[cols(chunk)].T
 
+    load_limits.wait()
     prepare(0)
 
     def step(s, carry):
@@ -210,10 +220,7 @@
 
     lax.fori_loop(0, dues[-1] + units, step, 0)
 
-    for level in range(1, count):
-        pltpu.make_async_copy(
-            mixed.at[level - 1], mixed.at[level - 1], send_sem.at[level - 1]
-        ).wait()
+    pltpu.make_async_copy(mixed, mixed, send_sem).wait()
     pltpu.make_async_copy(coef_ref, coef_ref, first_send).wait()
 
 
@@ -223,40 +230,41 @@
     )
     count = len(levels)
     depth, columns = coefficients.shape
-    chunks = columns // LANES
     units = columns // UNIT
     call = pl.pallas_call(
         functools.partial(kernel, levels),
         out_shape=jax.ShapeDtypeStruct(coefficients.shape, jnp.float32),
         in_specs=[
-            pl.BlockSpec(memory_space=pltpu.SMEM),
+            pl.BlockSpec(memory_space=pltpu.HBM),
             pl.BlockSpec(memory_space=pltpu.HBM),
             pl.BlockSpec(memory_space=pltpu.HBM),
         ],
         out_specs=pl.BlockSpec(memory_space=pltpu.VMEM),
         scratch_shapes=[
+            pltpu.SMEM((1, count), jnp.int32),
             pltpu.VMEM((count, depth, 2 * depth), jnp.float32),
             pltpu.VMEM((count, 2, 2 * depth, depth), jnp.bfloat16),
-            pltpu.VMEM((chunks, depth, LANES), jnp.float32),
-            pltpu.VMEM((chunks, depth, LANES), jnp.float32),
+            pltpu.VMEM((depth, columns), jnp.float32),
+            pltpu.VMEM((depth, columns), jnp.float32),
             pltpu.VMEM((2 * columns, depth), jnp.bfloat16),
             pltpu.VMEM((2 * columns, depth), jnp.bfloat16),
             pltpu.VMEM((count - 1, columns, depth), jnp.float32),
             pltpu.VMEM((count - 1, columns, depth), jnp.float32),
             pltpu.VMEM((columns, depth), jnp.float32),
+            pltpu.SemaphoreType.DMA,
             pltpu.SemaphoreType.DMA((count,)),
-            pltpu.SemaphoreType.DMA((chunks,)),
+            pltpu.SemaphoreType.DMA((3,)),
             pltpu.SemaphoreType.DMA,
-            pltpu.SemaphoreType.DMA((chunks,)),
-            pltpu.SemaphoreType.DMA((count - 1,)),
-            pltpu.SemaphoreType.DMA((count - 1, units)),
+            pltpu.SemaphoreType.DMA((3,)),
+            pltpu.SemaphoreType.DMA,
+            pltpu.SemaphoreType.DMA((count - 1, units // 2 + EDGE)),
         ],
         compiler_params=pltpu.CompilerParams(
             collective_id=0, has_side_effects=True, vmem_limit_bytes=55_000_000
         ),
         name="butterfly",
     )
-    return call(ranks.T, coefficients, transfer)
+    return call(pltpu.with_memory_space_constraint(ranks.T, pltpu.HBM), coefficients, transfer)
 
 
 def solution(mesh):

time: 68 us -> 66.2 us (0.974)
  Pallas kernels: 66.2 us -> 65.1 us
    pallas_call x1, Pallas kernels: 66.2 us -> 65.1 us  [per_device(): call(pltpu.with_memory_space_constraint(ranks.T, pltpu.HBM), coefficients...]
    unnamed x3 -> x1, local copies, waits for them, and re-layouts: 1.63 us -> 0.97 us
where the time goes in v2:
time: 66.2 us; the launch traced here: 66 us
  Pallas kernels  65.1 us (98%)
  local copies, waits for them, and re-layouts  0.97 us (1%)
    pallas_call x1, Pallas kernels, per_device(): call(pltpu.with_memory_space_constraint(ranks.T, pltpu.HBM), coefficients...  65.1 us

profile of v2, /device:TPU:0, one launch (start us, length us, event | category | flops | bytes accessed | tf_op | source)
XLA Modules:
  0.0 66.0 jit_solution(12441755671334218478)
XLA Ops:
  0.0 65.1 %butterfly.1 = f32[256,1024]{1,0:T(8,128)S(1)} custom-call(s32[1,5]{1,0:T(1,128)} %bitcast.1, f32[256,1024]{1,0:T(8,128)} %coef_ref.1, f32[5,256,512]{2,1,0:T(8,128)} %transfer_ref.1), custom_call_target="tpu_custom_call" | custom-call | tf_op jit(solution)/shard_map/butterfly/pallas_call | solution.py:267
  65.1 1.0 %copy.5 = f32[256,1024]{1,0:T(8,128)} copy(f32[256,1024]{1,0:T(8,128)S(1)} %butterfly.1) | data formatting | bytes 2097152

commit v3 on v2

--- a/solution.py
+++ b/solution.py
@@ -10,6 +10,7 @@
 LANES = 128
 UNIT = 32
 EDGE = LANES // UNIT
+TURN = 10
 LAGS = ((6, 6, 4), (6, 4, 4))
 
 
@@ -62,6 +63,9 @@
     def load_matrix(level):
         return pltpu.make_async_copy(transfer_ref.at[level], raw.at[level], raw_sem.at[level])
 
+    later = pl.ds(2, count - 2)
+    load_later = pltpu.make_async_copy(transfer_ref.at[later], raw.at[later], raw_sem.at[2])
+
     def send_first(part):
         return pltpu.make_async_remote_copy(
             src_ref=coef_ref.at[:, parts[part]],
@@ -83,7 +87,7 @@
             src_ref=mixed.at[level - 1, rows],
             dst_ref=landed.at[level - 1, rows],
             send_sem=send_sem,
-            recv_sem=recv_sem.at[level - 1, slot(unit)],
+            recv_sem=recv_sem.at[level - 1, slot(unit) % TURN],
             device_id=partners[level],
             device_id_type=pl.DeviceIdType.MESH,
         )
@@ -105,7 +109,10 @@
     load_part(2).start()
 
     def prepare(level):
-        load_matrix(level).wait()
+        if level < 2:
+            load_matrix(level).wait()
+        elif level == 2:
+            load_later.wait()
         keep = lax.broadcasted_iota(jnp.int32, (depth, depth), 0) < limits[0, level]
         for side, place in enumerate((places[level], 1 - places[level])):
             block = raw[level, :, pl.ds(pl.multiple_of(place * depth, depth), depth)]
@@ -203,8 +210,7 @@
 
         @pl.when(s == 0)
         def _():
-            for level in range(2, count):
-                load_matrix(level).start()
+            load_later.start()
 
         for level, due in enumerate(dues):
             if level:
@@ -252,12 +258,12 @@
             pltpu.VMEM((count - 1, columns, depth), jnp.float32),
             pltpu.VMEM((columns, depth), jnp.float32),
             pltpu.SemaphoreType.DMA,
-            pltpu.SemaphoreType.DMA((count,)),
+            pltpu.SemaphoreType.DMA((3,)),
             pltpu.SemaphoreType.DMA((3,)),
             pltpu.SemaphoreType.DMA,
             pltpu.SemaphoreType.DMA((3,)),
             pltpu.SemaphoreType.DMA,
-            pltpu.SemaphoreType.DMA((count - 1, units // 2 + EDGE)),
+            pltpu.SemaphoreType.DMA((count - 1, TURN)),
         ],
         compiler_params=pltpu.CompilerParams(
             collective_id=0, has_side_effects=True, vmem_limit_bytes=55_000_000

time: 66.2 us -> 65.8 us (level)
  no operation moved by 1% of the time
where the time goes in v3:
time: 65.8 us; the launch traced here: 65.7 us
  Pallas kernels  64.7 us (98%)
  local copies, waits for them, and re-layouts  0.97 us (1%)
    pallas_call x1, Pallas kernels, per_device(): call(pltpu.with_memory_space_constraint(ranks.T, pltpu.HBM), coefficients...  64.7 us

profile of v3, /device:TPU:0, one launch (start us, length us, event | category | flops | bytes accessed | tf_op | source)
XLA Modules:
  0.0 65.7 jit_solution(5934920747952706204)
XLA Ops:
  0.0 64.7 %butterfly.1 = f32[256,1024]{1,0:T(8,128)S(1)} custom-call(s32[1,5]{1,0:T(1,128)} %bitcast.1, f32[256,1024]{1,0:T(8,128)} %coef_ref.1, f32[5,256,512]{2,1,0:T(8,128)} %transfer_ref.1), custom_call_target="tpu_custom_call" | custom-call | tf_op jit(solution)/shard_map/butterfly/pallas_call | solution.py:273
  64.7 1.0 %copy.5 = f32[256,1024]{1,0:T(8,128)} copy(f32[256,1024]{1,0:T(8,128)S(1)} %butterfly.1) | data formatting | bytes 2097152

commit v4 on v3

--- a/solution.py
+++ b/solution.py
@@ -10,6 +10,7 @@
 LANES = 128
 UNIT = 32
 EDGE = LANES // UNIT
+HELD, HOLD = 3, 3
 TURN = 10
 LAGS = ((6, 6, 4), (6, 4, 4))
 
@@ -48,6 +49,7 @@
         places.append(upper)
         partners.append({axis: place + (1 - 2 * upper) * 2**bit})
     outer = (places[1] + places[2] + 1) % 2
+    hold = HOLD * outer
     dues = [inner + outer * (outside - inner) for _, _, (inner, outside) in levels]
 
     def cols(chunk):
@@ -213,7 +215,15 @@
             load_later.start()
 
         for level, due in enumerate(dues):
-            if level:
+            if level == 1:
+                at = s - due
+                late = at // (units - HELD + hold)
+
+                @pl.when((at >= 0) & (at < units + hold) & ((at < units - HELD) | (late > 0)))
+                def _():
+                    task(1, at - late * hold)
+
+            elif level:
                 @pl.when((s >= due) & (s < due + units))
                 def _():
                     task(level, s - due)

time: 65.8 us -> 64.8 us (0.985)
  Pallas kernels: 64.7 us -> 63.5 us
    pallas_call x1, Pallas kernels: 64.7 us -> 63.5 us  [per_device(): call(pltpu.with_memory_space_constraint(ranks.T, pltpu.HBM), coefficients...]
where the time goes in v4:
time: 64.8 us; the launch traced here: 64.4 us
  Pallas kernels  63.5 us (98%)
  local copies, waits for them, and re-layouts  0.97 us (1%)
    pallas_call x1, Pallas kernels, per_device(): call(pltpu.with_memory_space_constraint(ranks.T, pltpu.HBM), coefficients...  63.5 us

profile of v4, /device:TPU:0, one launch (start us, length us, event | category | flops | bytes accessed | tf_op | source)
XLA Modules:
  0.0 64.4 jit_solution(11399871192792860534)
XLA Ops:
  0.0 63.5 %butterfly.1 = f32[256,1024]{1,0:T(8,128)S(1)} custom-call(s32[1,5]{1,0:T(1,128)} %bitcast.1, f32[256,1024]{1,0:T(8,128)} %coef_ref.1, f32[5,256,512]{2,1,0:T(8,128)} %transfer_ref.1), custom_call_target="tpu_custom_call" | custom-call | tf_op jit(solution)/shard_map/butterfly/pallas_call | solution.py:283
  63.5 1.0 %copy.5 = f32[256,1024]{1,0:T(8,128)} copy(f32[256,1024]{1,0:T(8,128)S(1)} %butterfly.1) | data formatting | bytes 2097152

commit v5 on v4

--- a/solution.py
+++ b/solution.py
@@ -12,7 +12,7 @@
 EDGE = LANES // UNIT
 HELD, HOLD = 3, 3
 TURN = 10
-LAGS = ((6, 6, 4), (6, 4, 4))
+LAGS = ((4, 6, 4), (6, 4, 4))
 
 
 def split_rows(x):

time: 64.8 us -> 64.3 us (level)
  no operation moved by 1% of the time
where the time goes in v5:
time: 64.3 us; the launch traced here: 63.9 us
  Pallas kernels  62.9 us (98%)
  local copies, waits for them, and re-layouts  0.97 us (2%)
    pallas_call x1, Pallas kernels, per_device(): call(pltpu.with_memory_space_constraint(ranks.T, pltpu.HBM), coefficients...  62.9 us

profile of v5, /device:TPU:0, one launch (start us, length us, event | category | flops | bytes accessed | tf_op | source)
XLA Modules:
  0.0 63.9 jit_solution(207248841720076902)
XLA Ops:
  0.0 62.9 %butterfly.1 = f32[256,1024]{1,0:T(8,128)S(1)} custom-call(s32[1,5]{1,0:T(1,128)} %bitcast.1, f32[256,1024]{1,0:T(8,128)} %coef_ref.1, f32[5,256,512]{2,1,0:T(8,128)} %transfer_ref.1), custom_call_target="tpu_custom_call" | custom-call | tf_op jit(solution)/shard_map/butterfly/pallas_call | solution.py:283
  62.9 1.0 %copy.5 = f32[256,1024]{1,0:T(8,128)} copy(f32[256,1024]{1,0:T(8,128)S(1)} %butterfly.1) | data formatting | bytes 2097152

commit v6 on v5

--- a/solution.py
+++ b/solution.py
@@ -12,7 +12,7 @@
 EDGE = LANES // UNIT
 HELD, HOLD = 3, 3
 TURN = 10
-LAGS = ((4, 6, 4), (6, 4, 4))
+LAGS = ((4, 6, 3), (6, 4, 4))
 
 
 def split_rows(x):

time: 64.3 us -> 64.3 us (level)
  no operation moved by 1% of the time
where the time goes in v6:
time: 64.3 us; the launch traced here: 63.9 us
  Pallas kernels  62.9 us (98%)
  local copies, waits for them, and re-layouts  0.97 us (2%)
    pallas_call x1, Pallas kernels, per_device(): call(pltpu.with_memory_space_constraint(ranks.T, pltpu.HBM), coefficients...  62.9 us

profile of v6, /device:TPU:0, one launch (start us, length us, event | category | flops | bytes accessed | tf_op | source)
XLA Modules:
  0.0 63.9 jit_solution(14502030680273085899)
XLA Ops:
  0.0 62.9 %butterfly.1 = f32[256,1024]{1,0:T(8,128)S(1)} custom-call(s32[1,5]{1,0:T(1,128)} %bitcast.1, f32[256,1024]{1,0:T(8,128)} %coef_ref.1, f32[5,256,512]{2,1,0:T(8,128)} %transfer_ref.1), custom_call_target="tpu_custom_call" | custom-call | tf_op jit(solution)/shard_map/butterfly/pallas_call | solution.py:283
  62.9 1.0 %copy.5 = f32[256,1024]{1,0:T(8,128)} copy(f32[256,1024]{1,0:T(8,128)S(1)} %butterfly.1) | data formatting | bytes 2097152

commit v7 on v5

--- a/solution.py
+++ b/solution.py
@@ -105,10 +105,9 @@
         )
     load_part(1).start()
     pl.semaphore_wait(barrier, count)
-    for part in range(len(parts)):
+    for part in range(2):
         send_first(part).start()
     load_matrix(1).start()
-    load_part(2).start()
 
     def prepare(level):
         if level < 2:
@@ -212,6 +211,8 @@
 
         @pl.when(s == 0)
         def _():
+            send_first(2).start()
+            load_part(2).start()
             load_later.start()
 
         for level, due in enumerate(dues):

time: 64.3 us -> 64.3 us (level)
  no operation moved by 1% of the time
where the time goes in v7:
time: 64.3 us; the launch traced here: 63.9 us
  Pallas kernels  62.9 us (98%)
  local copies, waits for them, and re-layouts  0.97 us (2%)
    pallas_call x1, Pallas kernels, per_device(): call(pltpu.with_memory_space_constraint(ranks.T, pltpu.HBM), coefficients...  62.9 us

profile of v7, /device:TPU:0, one launch (start us, length us, event | category | flops | bytes accessed | tf_op | source)
XLA Modules:
  0.0 63.9 jit_solution(11696400330512087598)
XLA Ops:
  0.0 62.9 %butterfly.1 = f32[256,1024]{1,0:T(8,128)S(1)} custom-call(s32[1,5]{1,0:T(1,128)} %bitcast.1, f32[256,1024]{1,0:T(8,128)} %coef_ref.1, f32[5,256,512]{2,1,0:T(8,128)} %transfer_ref.1), custom_call_target="tpu_custom_call" | custom-call | tf_op jit(solution)/shard_map/butterfly/pallas_call | solution.py:284
  62.9 1.0 %copy.5 = f32[256,1024]{1,0:T(8,128)} copy(f32[256,1024]{1,0:T(8,128)S(1)} %butterfly.1) | data formatting | bytes 2097152

commit v8 on v7

--- a/solution.py
+++ b/solution.py
@@ -49,7 +49,7 @@
         places.append(upper)
         partners.append({axis: place + (1 - 2 * upper) * 2**bit})
     outer = (places[1] + places[2] + 1) % 2
-    hold = HOLD * outer
+    hold = HOLD * outer + (1 - outer) * places[0]
     dues = [inner + outer * (outside - inner) for _, _, (inner, outside) in levels]
 
     def cols(chunk):

time: 64.3 us -> 64.3 us (level)
  no operation moved by 1% of the time
where the time goes in v8:
time: 64.3 us; the launch traced here: 63.9 us
  Pallas kernels  62.9 us (98%)
  local copies, waits for them, and re-layouts  0.97 us (2%)
    pallas_call x1, Pallas kernels, per_device(): call(pltpu.with_memory_space_constraint(ranks.T, pltpu.HBM), coefficients...  62.9 us

profile of v8, /device:TPU:0, one launch (start us, length us, event | category | flops | bytes accessed | tf_op | source)
XLA Modules:
  0.0 63.9 jit_solution(15316006594226873135)
XLA Ops:
  0.0 62.9 %butterfly.1 = f32[256,1024]{1,0:T(8,128)S(1)} custom-call(s32[1,5]{1,0:T(1,128)} %bitcast.1, f32[256,1024]{1,0:T(8,128)} %coef_ref.1, f32[5,256,512]{2,1,0:T(8,128)} %transfer_ref.1), custom_call_target="tpu_custom_call" | custom-call | tf_op jit(solution)/shard_map/butterfly/pallas_call | solution.py:284
  62.9 1.0 %copy.5 = f32[256,1024]{1,0:T(8,128)} copy(f32[256,1024]{1,0:T(8,128)S(1)} %butterfly.1) | data formatting | bytes 2097152
